TPU v7x, 256 devices: a whole 4x4x8 slice. The times are simulated.
256 devices in a mesh: adapter: 64 (over x, z, core), tensor: 4 (over y).
Axes of the slice: x: 4, y: 4, z: 8, core: 2. Of those that a mesh axis runs over, the one named last changes fastest.
Arguments:
- activations: bfloat16 [32768, 4096], P('adapter', 'tensor'), may hold values from -6 to 6
- output_gradient: bfloat16 [32768, 4096], P('adapter', 'tensor'), may hold values from -6 to 6
- frozen_weight: bfloat16 [4096, 4096], P(None, 'tensor'), may hold values from -0.09375 to 0.09375
- adapter_down_weight: bfloat16 [8192, 4096], P('adapter', 'tensor'), may hold values from -0.09375 to 0.09375
- adapter_up_weight: bfloat16 [8192, 4096], P('adapter', 'tensor'), may hold values from -0.09375 to 0.09375
- adapter_slot_table: int32 [512], replicated, may hold values from 0 to 511, as said below
- group_adapter_index: int32 [64, 48], P('adapter'), may hold values from 0 to 511, as said below
- group_token_length: int32 [64, 48], P('adapter'), may hold values from 1 to 16, as said below
Outputs:
- input_gradient: bfloat16 [32768, 4096], P('adapter', 'tensor')
- down_grad: float32 [8192, 4096], P('adapter', 'tensor')
- up_grad: float32 [8192, 4096], P('adapter', 'tensor')
Inputs may be any that keep to these rules, and one draw needn't show every extreme that they name: `adapter_slot_table`: a permutation of the slots; slot k lies on adapter index k // 8. `group_adapter_index`: the adapters of one index's groups lie on distinct indices of the adapter axis; on every index one group of exactly 16 tokens uses an adapter stored on one index that is the same for all indices. `group_token_length`: each row sums to 512 and holds a group of exactly 16 tokens.
All inputs are finite; a program needn't handle non-finite values.
Results may differ from a plain program's by a relative error of at most 0.015.
Values may be sent and summed in bfloat16 or wider, within the bound.
A program may use at most 128 MiB of HBM per device.

v0:
```python
import jax
import jax.numpy as jnp
from jax import lax
from jax.sharding import PartitionSpec as P

ADAPTER_RANK = 16
ADP_DEV = 8
adapter_scale = 2.0


def rank_sums(down_part, up_part):
    return (
        lax.psum(down_part.astype(jnp.bfloat16), "tensor").astype(jnp.float32),
        lax.psum(up_part.astype(jnp.bfloat16), "tensor").astype(jnp.float32),
    )


def widen(mask, values):
    return jnp.where(mask[:, :, None], values[:, None, :], jnp.zeros((), values.dtype)).reshape(
        values.shape[0], mask.shape[1] * values.shape[1]
    )


def narrow(wide, mask):
    shaped = wide.reshape(wide.shape[0], mask.shape[1], ADAPTER_RANK)
    return jnp.sum(shaped * mask[:, :, None].astype(jnp.float32), axis=1)


def on_device(
    activations,
    output_gradient,
    frozen_weight,
    adapter_down_weight,
    adapter_up_weight,
    adapter_slot_table,
    group_adapter_index,
    group_token_length,
):
    tok_rows = activations.shape[0]
    devices = lax.axis_size("adapter")
    own_index = lax.axis_index("adapter")
    adapter_count = adapter_slot_table.shape[0]
    lengths = group_token_length[0]
    matched = group_adapter_index[0][:, None] == jnp.arange(adapter_count, dtype=jnp.int32)[None, :]
    group_slot = jnp.sum(jnp.where(matched, adapter_slot_table[None, :], 0), axis=1)
    group_owner = group_slot // ADP_DEV
    group_end = jnp.cumsum(lengths)
    positions = jnp.arange(tok_rows, dtype=jnp.int32)
    tok_group = jnp.sum((positions[:, None] >= group_end[None, :]).astype(jnp.int32), axis=1)
    group_onehot = tok_group[:, None] == jnp.arange(lengths.shape[0], dtype=jnp.int32)[None, :]
    tok_owner = jnp.sum(jnp.where(group_onehot, group_owner[None, :], 0), axis=1)
    gathered = lax.all_gather(jnp.stack([group_slot, lengths])[None], "adapter", axis=0, tiled=True)
    from_mine = gathered[:, 0] // ADP_DEV == own_index
    source_count = jnp.sum(jnp.where(from_mine, gathered[:, 1], 0), axis=1)
    source_local = jnp.sum(jnp.where(from_mine, gathered[:, 0] % ADP_DEV, 0), axis=1)
    source_hot = (source_local[:, None] == jnp.arange(ADP_DEV, dtype=jnp.int32)[None, :]) & (
        source_count > 0
    )[:, None]
    eye_rank = jnp.eye(ADAPTER_RANK, dtype=bool)
    selector = (source_hot[:, None, :, None] & eye_rank[None, :, None, :]).reshape(
        devices * ADAPTER_RANK, ADP_DEV * ADAPTER_RANK
    )
    selected_reduced = selector.astype(jnp.bfloat16)
    outgoing_down = jnp.dot(
        selected_reduced, adapter_down_weight, preferred_element_type=jnp.float32
    ).astype(jnp.bfloat16)
    outgoing_up = jnp.dot(
        selected_reduced, adapter_up_weight, preferred_element_type=jnp.float32
    ).astype(jnp.bfloat16)
    received_down, got_up = (
        lax.all_to_all(outgoing_down, "adapter", split_axis=0, concat_axis=0, tiled=True),
        lax.all_to_all(outgoing_up, "adapter", split_axis=0, concat_axis=0, tiled=True),
    )
    owner_hot = tok_owner[:, None] == jnp.arange(devices, dtype=jnp.int32)[None, :]
    down_wide = lax.dot_general(
        activations, received_down, (((1,), (1,)), ((), ())), preferred_element_type=jnp.float32
    )
    up_wide = lax.dot_general(
        output_gradient, got_up, (((1,), (1,)), ((), ())), preferred_element_type=jnp.float32
    )
    down_proj, up_proj = rank_sums(narrow(down_wide, owner_hot), narrow(up_wide, owner_hot))
    down_spread = widen(owner_hot, down_proj.astype(jnp.bfloat16))
    up_broadcast = widen(owner_hot, up_proj.astype(jnp.bfloat16))
    adapter_term = (
        adapter_scale * jnp.dot(up_broadcast, received_down, preferred_element_type=jnp.float32)
    ).astype(jnp.bfloat16)
    partial_down = adapter_scale * lax.dot_general(
        up_broadcast, activations, (((0,), (0,)), ((), ())), preferred_element_type=jnp.float32
    )
    partial_up = adapter_scale * lax.dot_general(
        down_spread, output_gradient, (((0,), (0,)), ((), ())), preferred_element_type=jnp.float32
    )
    back_down, back_up = (
        lax.all_to_all(
            partial_down.astype(jnp.bfloat16), "adapter", split_axis=0, concat_axis=0, tiled=True
        ).astype(partial_down.dtype),
        lax.all_to_all(
            partial_up.astype(jnp.bfloat16), "adapter", split_axis=0, concat_axis=0, tiled=True
        ).astype(partial_up.dtype),
    )
    select_full = selector.astype(jnp.float32)
    down_grad = lax.dot_general(
        select_full,
        back_down,
        (((0,), (0,)), ((), ())),
        precision=lax.Precision.HIGHEST,
        preferred_element_type=jnp.float32,
    )
    up_grad = lax.dot_general(
        select_full,
        back_up,
        (((0,), (0,)), ((), ())),
        precision=lax.Precision.HIGHEST,
        preferred_element_type=jnp.float32,
    )
    frozen_total_sum = lax.psum_scatter(
        lax.dot_general(
            frozen_weight,
            output_gradient,
            (((1,), (1,)), ((), ())),
            preferred_element_type=jnp.float32,
        ).astype(jnp.bfloat16),
        "tensor",
        scatter_dimension=0,
        tiled=True,
    ).astype(jnp.float32)
    input_gradient = (frozen_total_sum.T + adapter_term.astype(jnp.float32)).astype(jnp.bfloat16)
    return (input_gradient, down_grad, up_grad)


def solution(mesh):
    in_specs = (
        P("adapter", "tensor"),
        P("adapter", "tensor"),
        P(None, "tensor"),
        P("adapter", "tensor"),
        P("adapter", "tensor"),
        P(),
        P("adapter", None),
        P("adapter", None),
    )
    out_specs = (P("adapter", "tensor"), P("adapter", "tensor"), P("adapter", "tensor"))
    return jax.shard_map(
        on_device, mesh=mesh, in_specs=in_specs, out_specs=out_specs, check_vma=False
    )
```

profile of v0, /device:TPU:1, one launch (start us, length us, event | category | flops | bytes accessed | tf_op | source)
XLA Modules:
  0.0 331.1 jit_solution(9683461043637806220)
XLA Ops:
  7.2 1.0 select_reduce_fusion.1
  8.8 48.1 %all-gather.1 = s32[64,2,48]{2,1,0:T(2,128)S(1)} all-gather(s32[1,2,48]{2,1,0:T(2,128)S(1)} %add_bitcast_fusion), channel_id=2, replica_groups=mesh['adapter'=64,'tensor'=4] {'adapter'}, dimensions={0}, use_global_device_ids=true | all-gather | bytes 24960 | tf_op jit(solution)/shard_map/all_gather | solution.py:52
  57.8 1.5 and.72
  59.3 2.0 convolution_convert_fusion.1
  61.3 6.6 %all-to-all-start.1 = ((bf16[64,16,1024]{2,1,0:T(8,128)(2,1)}), bf16[64,16,1024]{2,1,0:T(8,128)(2,1)S(1)}, u32[]{:S(2)}, u32[]{:S(2)}) async-start(bf16[64,16,1024]{2,1,0:T(8,128)(2,1)} %bitcast.11), calls=%async_computation.2 | async-start | bytes 4194304 | tf_op jit(solution)/shard_map/all_to_all | solution.py:71
  67.9 2.0 convolution_convert_fusion.2
  70.0 49.2 %all-to-all-done.1 = bf16[64,16,1024]{2,1,0:T(8,128)(2,1)S(1)} async-done(((bf16[64,16,1024]{2,1,0:T(8,128)(2,1)}), bf16[64,16,1024]{2,1,0:T(8,128)(2,1)S(1)}, u32[]{:S(2)}, u32[]{:S(2)}) %all-to-all-start.1) | async-done | bytes 2097184 | tf_op jit(solution)/shard_map/all_to_all | solution.py:71
  119.2 6.1 %all-to-all-start = ((bf16[64,16,1024]{2,1,0:T(8,128)(2,1)}), bf16[64,16,1024]{2,1,0:T(8,128)(2,1)}, u32[]{:S(2)}, u32[]{:S(2)}) async-start(bf16[64,16,1024]{2,1,0:T(8,128)(2,1)} %bitcast.7), calls=%async_computation.1 | async-start | bytes 4194304 | tf_op jit(solution)/shard_map/all_to_all | solution.py:72
  125.9 3.9 %fusion.13 = f32[1024,512]{1,0:T(8,128)} fusion(bf16[1024,1024]{1,0:T(8,128)(2,1)S(1)} %bitcast.57, bf16[512,1024]{1,0:T(8,128)(2,1)} %param.8), kind=kOutput, calls=%fused_computation.47 | convolution fusion | flops 1073741824 | bytes 5242880 | tf_op jit(solution)/shard_map/dot_general | solution.py:75
  129.7 46.8 %all-to-all-done = bf16[64,16,1024]{2,1,0:T(8,128)(2,1)} async-done(((bf16[64,16,1024]{2,1,0:T(8,128)(2,1)}), bf16[64,16,1024]{2,1,0:T(8,128)(2,1)}, u32[]{:S(2)}, u32[]{:S(2)}) %all-to-all-start) | async-done | bytes 2097184 | tf_op jit(solution)/shard_map/all_to_all | solution.py:72
  176.5 3.0 fusion.11
  180.2 13.6 %all-reduce = (bf16[512,16]{0,1:T(8,128)(2,1)S(1)}, bf16[512,16]{0,1:T(8,128)(2,1)S(1)}) all-reduce(bf16[512,16]{0,1:T(8,128)(2,1)S(1)} %get-tuple-element.16, bf16[512,16]{0,1:T(8,128)(2,1)S(1)} %get-tuple-element.15), channel_id=1, replica_groups=mesh['adapter'=64,'tensor'=4] {'tensor'}, use_global_device_ids=true, to_apply=%region_8.9 | all-reduce | flops 16384 | bytes 65536 | tf_op jit(solution)/shard_map/psum | solution.py:14
  193.8 1.2 broadcast_select_fusion
  195.0 2.6 multiply_convert_fusion
  197.6 9.6 %all-to-all-start.3 = ((bf16[64,16,1024]{2,1,0:T(8,128)(2,1)}), bf16[64,16,1024]{2,1,0:T(8,128)(2,1)S(1)}, u32[]{:S(2)}, u32[]{:S(2)}) async-start(bf16[64,16,1024]{2,1,0:T(8,128)(2,1)} %bitcast.58), calls=%async_computation.4 | async-start | bytes 4194304 | tf_op jit(solution)/shard_map/all_to_all | solution.py:97
  207.4 9.6 %convolution_convert_fusion = bf16[4096,512]{1,0:T(8,128)(2,1)} fusion(bf16[4096,1024]{1,0:T(8,128)(2,1)} %param.10, bf16[512,1024]{1,0:T(8,128)(2,1)S(1)} %copy-done), kind=kOutput, calls=%fused_computation | convolution fusion | flops 4297064448 | bytes 13631488 | tf_op jit(solution)/shard_map/dot_general | solution.py:117
  217.0 4.2 %multiply_convert_fusion.1 = bf16[1024,1024]{1,0:T(8,128)(2,1)} fusion(bf16[512,1024]{0,1:T(8,128)(2,1)} %bitcast.62, bf16[512,1024]{1,0:T(8,128)(2,1)} %param.8), kind=kOutput, calls=%fused_computation.2 | convolution fusion | flops 1075838976 | bytes 4194304 | tf_op jit(solution)/shard_map/dot_general | solution.py:87
  221.2 37.2 %all-to-all-done.3 = bf16[64,16,1024]{2,1,0:T(8,128)(2,1)S(1)} async-done(((bf16[64,16,1024]{2,1,0:T(8,128)(2,1)}), bf16[64,16,1024]{2,1,0:T(8,128)(2,1)S(1)}, u32[]{:S(2)}, u32[]{:S(2)}) %all-to-all-start.3) | async-done | bytes 2097184 | tf_op jit(solution)/shard_map/all_to_all | solution.py:97
  258.4 6.0 %all-to-all-start.2 = ((bf16[64,16,1024]{2,1,0:T(8,128)(2,1)}), bf16[64,16,1024]{2,1,0:T(8,128)(2,1)}, u32[]{:S(2)}, u32[]{:S(2)}) async-start(bf16[64,16,1024]{2,1,0:T(8,128)(2,1)} %bitcast.59), calls=%async_computation.3 | async-start | bytes 4194304 | tf_op jit(solution)/shard_map/all_to_all | solution.py:94
  264.4 1.3 fusion.14
  265.7 49.9 %all-to-all-done.2 = bf16[64,16,1024]{2,1,0:T(8,128)(2,1)} async-done(((bf16[64,16,1024]{2,1,0:T(8,128)(2,1)}), bf16[64,16,1024]{2,1,0:T(8,128)(2,1)}, u32[]{:S(2)}, u32[]{:S(2)}) %all-to-all-start.2) | async-done | bytes 2097184 | tf_op jit(solution)/shard_map/all_to_all | solution.py:94
  315.6 2.9 fusion.12
  318.5 3.5 %fusion.1 = bf16[512,1024]{0,1:T(8,128)(2,1)} fusion(bf16[1024,512]{1,0:T(8,128)(2,1)} %reduce-scatter.2.cloned.1.call-done, bf16[64,16,1024]{2,1,0:T(8,128)(2,1)S(1)} %copy-done.2, pred[512,64]{0,1:T(8,128)(4,1)S(1)} %get-tuple-element.26, bf16[512,16]{0,1:T(8,128)(2,1)S(1)} %get-tuple-element.19), kind=kOutput, calls=%fused_computation.6 | convolution fusion | flops 1077411840 | bytes 4243456 | tf_op jit(solution)/shard_map/dot_general | solution.py:85
  322.0 2.3 copy.30
  (32 shorter events, 3.0 us)
Async XLA Ops:
  7.2 169.3 %copy-start = (bf16[512,1024]{1,0:T(8,128)(2,1)S(1)}, bf16[512,1024]{1,0:T(8,128)(2,1)}, u32[]{:S(2)}) copy-start(bf16[512,1024]{1,0:T(8,128)(2,1)} %param.9) | copy-start | bytes 3145732
  7.2 52.1 %copy-start.4 = (bf16[128,1024]{1,0:T(8,128)(2,1)S(1)}, bf16[128,1024]{1,0:T(8,128)(2,1)}, u32[]{:S(2)}) copy-start(bf16[128,1024]{1,0:T(8,128)(2,1)} %param.11) | copy-start | bytes 786436
  61.3 6.6 %copy-start.5 = (bf16[128,1024]{1,0:T(8,128)(2,1)S(1)}, bf16[128,1024]{1,0:T(8,128)(2,1)}, u32[]{:S(2)}) copy-start(bf16[128,1024]{1,0:T(8,128)(2,1)} %param.12) | copy-start | bytes 786436
  61.3 57.8 %all-to-all-start.1 = ((bf16[64,16,1024]{2,1,0:T(8,128)(2,1)}), bf16[64,16,1024]{2,1,0:T(8,128)(2,1)S(1)}, u32[]{:S(2)}, u32[]{:S(2)}) async-start(bf16[64,16,1024]{2,1,0:T(8,128)(2,1)} %bitcast.11), calls=%async_computation.2 | async-start | bytes 4194304 | tf_op jit(solution)/shard_map/all_to_all | solution.py:71
  119.2 6.7 %copy-start.1 = (bf16[64,16,1024]{2,1,0:T(8,128)(2,1)}, bf16[64,16,1024]{2,1,0:T(8,128)(2,1)S(1)}, u32[]{:S(2)}) copy-start(bf16[64,16,1024]{2,1,0:T(8,128)(2,1)S(1)} %all-to-all-done.1) | copy-start | bytes 6291460
  119.2 6.1 %copy-start.6 = (s32[1,48]{1,0:T(1,128)S(1)}, s32[1,48]{1,0:T(1,128)}, u32[]{:S(2)}) copy-start(s32[1,48]{1,0:T(1,128)} %param.15) | copy-start | bytes 580
  119.2 57.3 %all-to-all-start = ((bf16[64,16,1024]{2,1,0:T(8,128)(2,1)}), bf16[64,16,1024]{2,1,0:T(8,128)(2,1)}, u32[]{:S(2)}, u32[]{:S(2)}) async-start(bf16[64,16,1024]{2,1,0:T(8,128)(2,1)} %bitcast.7), calls=%async_computation.1 | async-start | bytes 4194304 | tf_op jit(solution)/shard_map/all_to_all | solution.py:72
  176.5 3.0 copy-start.3
  197.6 60.8 %all-to-all-start.3 = ((bf16[64,16,1024]{2,1,0:T(8,128)(2,1)}), bf16[64,16,1024]{2,1,0:T(8,128)(2,1)S(1)}, u32[]{:S(2)}, u32[]{:S(2)}) async-start(bf16[64,16,1024]{2,1,0:T(8,128)(2,1)} %bitcast.58), calls=%async_computation.4 | async-start | bytes 4194304 | tf_op jit(solution)/shard_map/all_to_all | solution.py:97
  207.2 111.3 %reduce-scatter.2.cloned.1.call-start = ((), (), s32[]{:S(2)}) async-start(), calls=%async_computation.5 | async-start | bytes 5242880 | tf_op jit(solution)/shard_map/reduce_scatter | solution.py:116
  258.4 57.2 %all-to-all-start.2 = ((bf16[64,16,1024]{2,1,0:T(8,128)(2,1)}), bf16[64,16,1024]{2,1,0:T(8,128)(2,1)}, u32[]{:S(2)}, u32[]{:S(2)}) async-start(bf16[64,16,1024]{2,1,0:T(8,128)(2,1)} %bitcast.59), calls=%async_computation.3 | async-start | bytes 4194304 | tf_op jit(solution)/shard_map/all_to_all | solution.py:94
  265.7 52.8 %copy-start.2 = (bf16[64,16,1024]{2,1,0:T(8,128)(2,1)S(1)}, bf16[64,16,1024]{2,1,0:T(8,128)(2,1)}, u32[]{:S(2)}) copy-start(bf16[64,16,1024]{2,1,0:T(8,128)(2,1)} %copy-done.1) | copy-start | bytes 6291460
Sparse Core Ops, SparseCore 0:
  217.1 48.8 reduce-scatter.1
where the time goes:
time: 332 us; the launch traced here: 331 us
  waiting for transfers between devices  183 us (55%)
  blocking collectives  61.7 us (19%)
  matrix products  35 us (11%)
  starting transfers between devices  28.5 us (9%)
  between operations  14.2 us (4%)
  other arithmetic  4.68 us (1%)
  local copies, waits for them, and re-layouts  3.91 us (1%)
    all_to_all x1, waiting for transfers between devices, on_device(): lax.all_to_all(partial_down.astype(jnp.bfloat16), 'adapter', split_axis=0...  49.9 us
    all_to_all x1, waiting for transfers between devices, on_device(): lax.all_to_all(outgoing_down, 'adapter', split_axis=0, concat_axis=0, til...  49.2 us
    all_gather x1, blocking collectives, on_device(): lax.all_gather(jnp.stack([group_slot, lengths])[None], 'adapter', axis=0,...  48.1 us
    all_to_all x1, waiting for transfers between devices, on_device(): lax.all_to_all(outgoing_up, 'adapter', split_axis=0, concat_axis=0, tiled...  46.8 us
    all_to_all x1, waiting for transfers between devices, on_device(): lax.all_to_all(partial_up.astype(jnp.bfloat16), 'adapter', split_axis=0,...  37.2 us
    psum x1, blocking collectives, rank_sums(): lax.psum(up_part.astype(jnp.bfloat16), 'tensor').astype(jnp.float32)  13.6 us
    all_to_all x1, starting transfers between devices, on_device(): lax.all_to_all(partial_up.astype(jnp.bfloat16), 'adapter', split_axis=0,...  9.57 us
    dot_general x1, matrix products, on_device(): lax.dot_general(frozen_weight, output_gradient, (((1,), (1,)), ((), ())),...  9.56 us
  transfers between devices with their start and end apart: 5, of which 4 were waited for; matrix products, arithmetic and copies ran while one was open for 7% of the time, Pallas kernels for 0%

commit v1 on v0

--- a/solution.py
+++ b/solution.py
@@ -11,7 +11,7 @@
 def rank_sums(down_part, up_part):
     return (
         lax.psum(down_part.astype(jnp.bfloat16), "tensor").astype(jnp.float32),
-        lax.psum(up_part.astype(jnp.bfloat16), "tensor").astype(jnp.float32),
+        jnp.sum(lax.all_gather(up_part.astype(jnp.bfloat16), "tensor"), axis=0).astype(jnp.float32),
     )
 
 

time: 332 us -> 344 us (1.036)
  blocking collectives: 61.7 us -> 70.8 us
    all_gather x0 -> x1, blocking collectives: none -> 9.49 us  [rank_sums(): lax.all_gather(up_part.astype(jnp.bfloat16), 'tensor')]
where the time goes in v1:
time: 344 us; the launch traced here: 343 us
  waiting for transfers between devices  183 us (53%)
  blocking collectives  70.8 us (21%)
  matrix products  35 us (10%)
  starting transfers between devices  31.2 us (9%)
  between operations  14.2 us (4%)
  other arithmetic  4.76 us (1%)
  local copies, waits for them, and re-layouts  3.94 us (1%)
    all_to_all x1, waiting for transfers between devices, on_device(): lax.all_to_all(partial_down.astype(jnp.bfloat16), 'adapter', split_axis=0...  49.9 us
    all_to_all x1, waiting for transfers between devices, on_device(): lax.all_to_all(outgoing_down, 'adapter', split_axis=0, concat_axis=0, til...  49.2 us
    all_gather x1, blocking collectives, on_device(): lax.all_gather(jnp.stack([group_slot, lengths])[None], 'adapter', axis=0,...  48.1 us
    all_to_all x1, waiting for transfers between devices, on_device(): lax.all_to_all(outgoing_up, 'adapter', split_axis=0, concat_axis=0, tiled...  46.8 us
    all_to_all x1, waiting for transfers between devices, on_device(): lax.all_to_all(partial_up.astype(jnp.bfloat16), 'adapter', split_axis=0,...  37.2 us
    psum x1, blocking collectives, rank_sums(): lax.psum(down_part.astype(jnp.bfloat16), 'tensor').astype(jnp.float32)  13.1 us
    all_to_all x1, starting transfers between devices, on_device(): lax.all_to_all(partial_up.astype(jnp.bfloat16), 'adapter', split_axis=0,...  12.2 us
    dot_general x1, matrix products, on_device(): lax.dot_general(frozen_weight, output_gradient, (((1,), (1,)), ((), ())),...  9.56 us
  transfers between devices with their start and end apart: 5, of which 4 were waited for; matrix products, arithmetic and copies ran while one was open for 7% of the time, Pallas kernels for 0%

profile of v1, /device:TPU:1, one launch (start us, length us, event | category | flops | bytes accessed | tf_op | source)
XLA Modules:
  0.0 342.9 jit_solution(701613480540861170)
XLA Ops:
  8.8 48.1 %all-gather.2 = s32[64,2,48]{2,1,0:T(2,128)S(1)} all-gather(s32[1,2,48]{2,1,0:T(2,128)S(1)} %add_bitcast_fusion), channel_id=2, replica_groups=mesh['adapter'=64,'tensor'=4] {'adapter'}, dimensions={0}, use_global_device_ids=true | all-gather | bytes 24960 | tf_op jit(solution)/shard_map/all_gather | solution.py:52
  57.8 1.5 and.72
  59.3 2.0 convolution_convert_fusion.1
  61.3 6.6 %all-to-all-start.1 = ((bf16[64,16,1024]{2,1,0:T(8,128)(2,1)}), bf16[64,16,1024]{2,1,0:T(8,128)(2,1)S(1)}, u32[]{:S(2)}, u32[]{:S(2)}) async-start(bf16[64,16,1024]{2,1,0:T(8,128)(2,1)} %bitcast.11), calls=%async_computation.2 | async-start | bytes 4194304 | tf_op jit(solution)/shard_map/all_to_all | solution.py:71
  67.9 2.0 convolution_convert_fusion.2
  70.0 49.2 %all-to-all-done.1 = bf16[64,16,1024]{2,1,0:T(8,128)(2,1)S(1)} async-done(((bf16[64,16,1024]{2,1,0:T(8,128)(2,1)}), bf16[64,16,1024]{2,1,0:T(8,128)(2,1)S(1)}, u32[]{:S(2)}, u32[]{:S(2)}) %all-to-all-start.1) | async-done | bytes 2097184 | tf_op jit(solution)/shard_map/all_to_all | solution.py:71
  119.2 6.1 %all-to-all-start = ((bf16[64,16,1024]{2,1,0:T(8,128)(2,1)}), bf16[64,16,1024]{2,1,0:T(8,128)(2,1)}, u32[]{:S(2)}, u32[]{:S(2)}) async-start(bf16[64,16,1024]{2,1,0:T(8,128)(2,1)} %bitcast.7), calls=%async_computation.1 | async-start | bytes 4194304 | tf_op jit(solution)/shard_map/all_to_all | solution.py:72
  125.9 3.9 %fusion.13 = f32[1024,512]{1,0:T(8,128)} fusion(bf16[1024,1024]{1,0:T(8,128)(2,1)S(1)} %bitcast.59, bf16[512,1024]{1,0:T(8,128)(2,1)} %param.8), kind=kOutput, calls=%fused_computation.47 | convolution fusion | flops 1073741824 | bytes 5242880 | tf_op jit(solution)/shard_map/dot_general | solution.py:75
  129.7 46.8 %all-to-all-done = bf16[64,16,1024]{2,1,0:T(8,128)(2,1)} async-done(((bf16[64,16,1024]{2,1,0:T(8,128)(2,1)}), bf16[64,16,1024]{2,1,0:T(8,128)(2,1)}, u32[]{:S(2)}, u32[]{:S(2)}) %all-to-all-start) | async-done | bytes 2097184 | tf_op jit(solution)/shard_map/all_to_all | solution.py:72
  176.5 3.0 fusion.11
  180.2 9.5 %all-gather.1 = bf16[2048,16]{0,1:T(8,128)(2,1)S(1)} all-gather(bf16[512,16]{0,1:T(8,128)(2,1)S(1)} %get-tuple-element.16), channel_id=3, replica_groups=mesh['adapter'=64,'tensor'=4] {'tensor'}, dimensions={0}, use_global_device_ids=true | all-gather | bytes 81920 | tf_op jit(solution)/shard_map/all_gather | solution.py:14
  189.7 13.1 %psum.7 = bf16[512,16]{0,1:T(8,128)(2,1)S(1)} all-reduce(bf16[512,16]{0,1:T(8,128)(2,1)S(1)} %get-tuple-element.15), channel_id=1, replica_groups=mesh['adapter'=64,'tensor'=4] {'tensor'}, use_global_device_ids=true, to_apply=%region_10.11 | all-reduce | flops 8192 | bytes 32768 | tf_op jit(solution)/shard_map/psum | solution.py:13
  203.0 1.2 broadcast_select_fusion
  204.1 2.6 multiply_convert_fusion
  206.7 12.2 %all-to-all-start.3 = ((bf16[64,16,1024]{2,1,0:T(8,128)(2,1)}), bf16[64,16,1024]{2,1,0:T(8,128)(2,1)S(1)}, u32[]{:S(2)}, u32[]{:S(2)}) async-start(bf16[64,16,1024]{2,1,0:T(8,128)(2,1)} %bitcast.60), calls=%async_computation.4 | async-start | bytes 4194304 | tf_op jit(solution)/shard_map/all_to_all | solution.py:97
  219.2 9.6 %convolution_convert_fusion = bf16[4096,512]{1,0:T(8,128)(2,1)} fusion(bf16[4096,1024]{1,0:T(8,128)(2,1)} %param.10, bf16[512,1024]{1,0:T(8,128)(2,1)S(1)} %copy-done), kind=kOutput, calls=%fused_computation | convolution fusion | flops 4297064448 | bytes 13631488 | tf_op jit(solution)/shard_map/dot_general | solution.py:117
  228.8 4.2 %multiply_convert_fusion.1 = bf16[1024,1024]{1,0:T(8,128)(2,1)} fusion(bf16[512,1024]{0,1:T(8,128)(2,1)} %bitcast.64, bf16[512,1024]{1,0:T(8,128)(2,1)} %param.8), kind=kOutput, calls=%fused_computation.2 | convolution fusion | flops 1075838976 | bytes 4194304 | tf_op jit(solution)/shard_map/dot_general | solution.py:87
  233.0 37.2 %all-to-all-done.3 = bf16[64,16,1024]{2,1,0:T(8,128)(2,1)S(1)} async-done(((bf16[64,16,1024]{2,1,0:T(8,128)(2,1)}), bf16[64,16,1024]{2,1,0:T(8,128)(2,1)S(1)}, u32[]{:S(2)}, u32[]{:S(2)}) %all-to-all-start.3) | async-done | bytes 2097184 | tf_op jit(solution)/shard_map/all_to_all | solution.py:97
  270.2 6.0 %all-to-all-start.2 = ((bf16[64,16,1024]{2,1,0:T(8,128)(2,1)}), bf16[64,16,1024]{2,1,0:T(8,128)(2,1)}, u32[]{:S(2)}, u32[]{:S(2)}) async-start(bf16[64,16,1024]{2,1,0:T(8,128)(2,1)} %bitcast.61), calls=%async_computation.3 | async-start | bytes 4194304 | tf_op jit(solution)/shard_map/all_to_all | solution.py:94
  276.2 1.3 fusion.14
  277.5 49.9 %all-to-all-done.2 = bf16[64,16,1024]{2,1,0:T(8,128)(2,1)} async-done(((bf16[64,16,1024]{2,1,0:T(8,128)(2,1)}), bf16[64,16,1024]{2,1,0:T(8,128)(2,1)}, u32[]{:S(2)}, u32[]{:S(2)}) %all-to-all-start.2) | async-done | bytes 2097184 | tf_op jit(solution)/shard_map/all_to_all | solution.py:94
  327.4 2.9 fusion.12
  330.3 3.5 %fusion.1 = bf16[512,1024]{0,1:T(8,128)(2,1)} fusion(bf16[1024,512]{1,0:T(8,128)(2,1)} %reduce-scatter.2.cloned.1.call-done, bf16[64,16,1024]{2,1,0:T(8,128)(2,1)S(1)} %copy-done.2, pred[512,64]{0,1:T(8,128)(4,1)S(1)} %get-tuple-element.24, bf16[512,16]{0,1:T(8,128)(2,1)S(1)} %reduce_sum.84), kind=kOutput, calls=%fused_computation.6 | convolution fusion | flops 1077411840 | bytes 4243456 | tf_op jit(solution)/shard_map/dot_general | solution.py:85
  333.8 2.3 copy.30
  (35 shorter events, 4.1 us)
Async XLA Ops:
  7.2 169.3 %copy-start = (bf16[512,1024]{1,0:T(8,128)(2,1)S(1)}, bf16[512,1024]{1,0:T(8,128)(2,1)}, u32[]{:S(2)}) copy-start(bf16[512,1024]{1,0:T(8,128)(2,1)} %param.9) | copy-start | bytes 3145732
  7.2 52.1 %copy-start.4 = (bf16[128,1024]{1,0:T(8,128)(2,1)S(1)}, bf16[128,1024]{1,0:T(8,128)(2,1)}, u32[]{:S(2)}) copy-start(bf16[128,1024]{1,0:T(8,128)(2,1)} %param.11) | copy-start | bytes 786436
  61.3 6.6 %copy-start.5 = (bf16[128,1024]{1,0:T(8,128)(2,1)S(1)}, bf16[128,1024]{1,0:T(8,128)(2,1)}, u32[]{:S(2)}) copy-start(bf16[128,1024]{1,0:T(8,128)(2,1)} %param.12) | copy-start | bytes 786436
  61.3 57.8 %all-to-all-start.1 = ((bf16[64,16,1024]{2,1,0:T(8,128)(2,1)}), bf16[64,16,1024]{2,1,0:T(8,128)(2,1)S(1)}, u32[]{:S(2)}, u32[]{:S(2)}) async-start(bf16[64,16,1024]{2,1,0:T(8,128)(2,1)} %bitcast.11), calls=%async_computation.2 | async-start | bytes 4194304 | tf_op jit(solution)/shard_map/all_to_all | solution.py:71
  119.2 6.7 %copy-start.1 = (bf16[64,16,1024]{2,1,0:T(8,128)(2,1)}, bf16[64,16,1024]{2,1,0:T(8,128)(2,1)S(1)}, u32[]{:S(2)}) copy-start(bf16[64,16,1024]{2,1,0:T(8,128)(2,1)S(1)} %all-to-all-done.1) | copy-start | bytes 6291460
  119.2 6.1 %copy-start.6 = (s32[1,48]{1,0:T(1,128)S(1)}, s32[1,48]{1,0:T(1,128)}, u32[]{:S(2)}) copy-start(s32[1,48]{1,0:T(1,128)} %param.15) | copy-start | bytes 580
  119.2 57.3 %all-to-all-start = ((bf16[64,16,1024]{2,1,0:T(8,128)(2,1)}), bf16[64,16,1024]{2,1,0:T(8,128)(2,1)}, u32[]{:S(2)}, u32[]{:S(2)}) async-start(bf16[64,16,1024]{2,1,0:T(8,128)(2,1)} %bitcast.7), calls=%async_computation.1 | async-start | bytes 4194304 | tf_op jit(solution)/shard_map/all_to_all | solution.py:72
  176.5 3.0 copy-start.3
  206.7 63.5 %all-to-all-start.3 = ((bf16[64,16,1024]{2,1,0:T(8,128)(2,1)}), bf16[64,16,1024]{2,1,0:T(8,128)(2,1)S(1)}, u32[]{:S(2)}, u32[]{:S(2)}) async-start(bf16[64,16,1024]{2,1,0:T(8,128)(2,1)} %bitcast.60), calls=%async_computation.4 | async-start | bytes 4194304 | tf_op jit(solution)/shard_map/all_to_all | solution.py:97
  219.0 111.3 %reduce-scatter.2.cloned.1.call-start = ((), (), s32[]{:S(2)}) async-start(), calls=%async_computation.5 | async-start | bytes 5242880 | tf_op jit(solution)/shard_map/reduce_scatter | solution.py:116
  270.2 57.2 %all-to-all-start.2 = ((bf16[64,16,1024]{2,1,0:T(8,128)(2,1)}), bf16[64,16,1024]{2,1,0:T(8,128)(2,1)}, u32[]{:S(2)}, u32[]{:S(2)}) async-start(bf16[64,16,1024]{2,1,0:T(8,128)(2,1)} %bitcast.61), calls=%async_computation.3 | async-start | bytes 4194304 | tf_op jit(solution)/shard_map/all_to_all | solution.py:94
  277.5 52.8 %copy-start.2 = (bf16[64,16,1024]{2,1,0:T(8,128)(2,1)S(1)}, bf16[64,16,1024]{2,1,0:T(8,128)(2,1)}, u32[]{:S(2)}) copy-start(bf16[64,16,1024]{2,1,0:T(8,128)(2,1)} %copy-done.1) | copy-start | bytes 6291460
Sparse Core Ops, SparseCore 0:
  228.9 48.2 reduce-scatter.1
